TPU v7x, 256 devices: a whole 4x4x8 slice. The times are simulated.
256 devices in a mesh: gx: 8 (over z), gy: 8 (over x, core), gz: 4 (over y).
Axes of the slice: x: 4, y: 4, z: 8, core: 2. Of those that a mesh axis runs over, the one named last changes fastest.
Arguments:
- velocity: float32 [3, 64, 128, 1024], P(None, 'gz', 'gx', 'gy'), may hold values from -20 to 20
- owner: int32 [262144, 1], P(('gx', 'gy', 'gz')), may hold values from 0 to 63; in each aligned block of 1024 rows (0 to 1023, 1024 to 2047, ...) at most 64 rows name the same one
- cell_x: int32 [262144], P(('gx', 'gy', 'gz')), may hold values from 0 to 14
- cell_y: int32 [262144], P(('gx', 'gy', 'gz')), may hold values from 0 to 126
- cell_z: int32 [262144], P(('gx', 'gy', 'gz')), may hold values from 0 to 14
- query_weights: float32 [3, 262144], P(None, ('gx', 'gy', 'gz')), may hold values from 0 to 1
Outputs:
- query_stress: float32 [6, 262144], P(None, ('gx', 'gy', 'gz'))
Inputs may be any that keep to these rules, and one draw needn't show every extreme that they name: Among the queries held by one device, at most 64 name the same owner, and in every draw some owner is named by exactly 64 of them. `cell_x`: the corner cell plus one stays in the same brick.
All inputs are finite; a program needn't handle non-finite values.
Results may differ from a plain program's by a relative error of at most 0.0003.
Values sent between devices are 32-bit elements; how exact they have to be, the bound alone decides.
A program may use at most 64 MiB of HBM per device.

v0:
```python
import jax
import jax.numpy as jnp
from jax import lax
from jax.sharding import PartitionSpec as P

FW = 32
PAIRS = ((0, 0), (0, 1), (0, 2), (1, 1), (1, 2), (2, 2))


def padded(x, sides, width):
    for axis, dim in sides:
        devices, length = (lax.axis_size(axis), x.shape[dim])
        up = [(i, (i + 1) % devices) for i in range(devices)]
        down = [(j, i) for i, j in up]
        last = lax.slice_in_dim(x, length - width, length, axis=dim)
        initial = lax.slice_in_dim(x, 0, width, axis=dim)
        before = lax.ppermute(last, axis, up)
        after = lax.ppermute(initial, axis, down)
        x = jnp.concatenate([before, x, after], axis=dim)
    return x


def taps(radius, width):
    offsets = jnp.arange(2 * radius + 1).astype(jnp.float32) - radius
    values = jnp.exp(-6.0 * offsets * offsets / (width * width))
    return values / jnp.sum(values)


def band(length, radius, width):
    weights = taps(radius, width)
    rows = jnp.arange(length + 2 * radius)[:, None]
    cols = jnp.arange(length)[None, :]
    offset = rows - cols
    inside = (offset >= 0) & (offset <= 2 * radius)
    picked = weights[jnp.clip(offset, 0, 2 * radius)]
    return jnp.where(inside, picked, jnp.zeros_like(picked))


def filter_x(fields, matrix):
    return jnp.einsum("czpy,pq->czqy", fields, matrix, precision=lax.Precision.HIGHEST)


def filter_y(fields, matrix):
    return jnp.einsum("czxp,pq->czxq", fields, matrix, precision=lax.Precision.HIGHEST)


def interpolate(flat_stress, index, weight, size_x, size_y):
    shape = index.shape[1:]
    base = index[0].reshape(-1)
    offsets = weight.reshape(3, -1)
    wx = offsets[0]
    wy = offsets[1]
    wz = offsets[2]
    total = jnp.zeros((6, base.shape[0]), jnp.float32)
    for dz in (0, 1):
        for dx in (0, 1):
            for dy in (0, 1):
                corner = base + dz * size_x * size_y + dx * size_y + dy
                values = jnp.take(flat_stress, corner, axis=1)
                term = (
                    (wz if dz else 1.0 - wz) * (wx if dx else 1.0 - wx) * (wy if dy else 1.0 - wy)
                )
                total = total + term[None, :] * values
    return total.reshape((6,) + shape)


def on_device(velocity, owner, cell_x, cell_y, cell_z, query_weights):
    radius = FW // 2
    size_z = velocity.shape[1]
    size_x = velocity.shape[2]
    size_y = velocity.shape[3]
    layered = padded(velocity, (("gz", 1),), radius)
    band_z = band(size_z, radius, FW)
    band_x = band(size_x, radius, FW)
    band_y = band(size_y, radius, FW)
    fields = []
    for comp in range(3):
        fields.append(
            jnp.einsum("pxy,pz->zxy", layered[comp], band_z, precision=lax.Precision.HIGHEST)
        )
    for first, second in PAIRS:
        product = layered[first] * layered[second]
        fields.append(jnp.einsum("pxy,pz->zxy", product, band_z, precision=lax.Precision.HIGHEST))
    stacked = jnp.stack(fields)
    margined = padded(stacked, (("gx", 2), ("gy", 3)), radius)
    filtered = filter_y(filter_x(margined, band_x), band_y)
    stress = jnp.stack(
        [
            filtered[3 + k] - filtered[first] * filtered[second]
            for k, (first, second) in enumerate(PAIRS)
        ]
    )
    flat_stress = stress.reshape(6, -1)
    bricks_x = lax.axis_size("gx")
    bricks_y = lax.axis_size("gy")
    owners = bricks_x * bricks_y
    count = owner.shape[0]
    capacity = 4 * count // owners
    target = owner[:, 0]
    order = jnp.argsort(target, stable=True)
    sorted_target = target[order]
    tally = jnp.sum(
        (target[:, None] == jnp.arange(owners, dtype=jnp.int32)[None, :]).astype(jnp.int32), axis=0
    )
    starts = jnp.cumsum(tally) - tally
    sorted_rank = jnp.arange(count, dtype=jnp.int32) - starts[sorted_target]
    rank = jnp.zeros((count,), jnp.int32).at[order].set(sorted_rank)
    slot = target * capacity + rank
    local_cell = (cell_z * size_x + cell_x) * size_y + cell_y
    send_index = jnp.zeros((owners * capacity,), jnp.int32).at[slot].set(local_cell)
    send_weight = jnp.zeros((3, owners * capacity), jnp.float32).at[:, slot].set(query_weights)
    values = interpolate(
        flat_stress,
        lax.all_to_all(
            send_index.reshape(1, owners, capacity),
            ("gx", "gy"),
            split_axis=1,
            concat_axis=1,
            tiled=True,
        ),
        lax.all_to_all(
            send_weight.reshape(3, owners, capacity),
            ("gx", "gy"),
            split_axis=1,
            concat_axis=1,
            tiled=True,
        ),
        size_x,
        size_y,
    )
    returned = lax.all_to_all(values, ("gx", "gy"), split_axis=1, concat_axis=1, tiled=True)
    flat_back = returned.reshape(6, owners * capacity)
    return jnp.take(flat_back, slot, axis=1)


def solution(mesh):
    placed = (
        P(None, "gz", "gx", "gy"),
        P(("gx", "gy", "gz"), None),
        P(("gx", "gy", "gz")),
        P(("gx", "gy", "gz")),
        P(("gx", "gy", "gz")),
        P(None, ("gx", "gy", "gz")),
    )
    return jax.shard_map(
        on_device,
        mesh=mesh,
        in_specs=placed,
        out_specs=P(None, ("gx", "gy", "gz")),
        check_vma=False,
    )
```

profile of v0, /device:TPU:1, one launch (start us, length us, event | category | flops | bytes accessed | tf_op | source)
XLA Modules:
  0.0 546.4 jit_solution(7970189455837514659)
XLA Ops:
  0.0 1.1 copy.108
  1.1 2.2 collective-permute-start
  3.3 1.5 collective-permute-start.1
  4.9 0.8 convert_reduce_fusion
  6.0 0.7 fusion.87
  6.8 0.7 fusion.88
  7.4 5.1 sort.17
  12.6 4.5 gather_fusion
  17.1 4.3 compare_select_fusion.11
  21.4 0.7 fusion.85
  22.8 0.7 fusion.86
  23.5 0.7 compare_reduce_fusion.56
  24.2 0.7 broadcast_divide_fusion
  24.9 4.8 gather_fusion.1
  33.3 5.7 %collective-permute-start.3 = (f32[9,16,16,128]{3,1,2,0:T(8,128)S(1)}, f32[9,16,16,128]{3,1,2,0:T(8,128)}, u32[]{:S(2)}, u32[]{:S(2)}) collective-permute-start(f32[9,16,16,128]{3,1,2,0:T(8,128)S(1)} %fusion.4), channel_id=1, source_target_pairs={{32,0},{64,32},{96,64},{128,96},{160,128},{192,160},{224,192},{0,2... | collective-permute-start | bytes 3538952 | tf_op jit(solution)/shard_map/ppermute | solution.py:18
  38.9 35.9 %select_subtract_fusion = s32[1024]{0:T(1024)S(1)} fusion(pred[1024]{0:T(1024)(128)(4,1)S(1)} %get-tuple-element.67, pred[1024]{0:T(1024)(128)(4,1)S(1)} %get-tuple-element.66, pred[1024]{0:T(1024)(128)(4,1)S(1)} %get-tuple-element.65, pred[1024]{0:T(1024)(128)(4,1)S(1)} %get-tuple-element.64, pred[1024]{0:T(1024)(128)(4,1)S(1)} %get-tuple-element.63, ...), kind=kLoop, calls=%fused_computation.212 | loop fusion | flops 59392 | bytes 66788 | tf_op jit(solution)/shard_map/sub | solution.py:106
  74.9 4.3 scatter_custom_fusion
  79.8 4.3 scatter_custom_fusion.2
  84.2 0.7 reshape.232
  84.9 9.6 %all-to-all-start.1 = ((s32[1,64,64]{2,0,1:T(1,128)}), s32[1,64,64]{2,0,1:T(1,128)S(1)}, u32[]{:S(2)}, u32[]{:S(2)}) async-start(s32[1,64,64]{2,0,1:T(1,128)} %reshape.232), calls=%async_computation.1 | async-start | bytes 65536 | tf_op jit(solution)/shard_map/all_to_all | solution.py:114
  94.5 209.5 %gather_fusion.2 = f32[20480]{0:T(1024)} fusion(f32[33]{0:T(128)S(1)} %broadcast_divide_fusion, s32[20480]{0:T(1024)S(1)} %fusion.29), kind=kCustom, calls=%fused_computation.10 | custom fusion | bytes 245760 | tf_op jit(solution)/shard_map/gather | solution.py:35
  304.0 1.0 copy.106
  305.0 4.0 scatter_custom_fusion.1
  309.0 0.7 copy.107
  309.7 0.8 reshape.699
  310.5 10.5 %all-to-all-start = ((f32[64,1,192]{2,1,0:T(1,128)}), f32[64,1,192]{2,1,0:T(1,128)}, u32[]{:S(2)}, u32[]{:S(2)}) async-start(f32[64,1,192]{2,1,0:T(1,128)} %reshape.699), calls=%async_computation | async-start | bytes 131072 | tf_op jit(solution)/shard_map/all_to_all | solution.py:121
  321.5 0.7 reduce.130
  322.3 0.7 fusion.53
  323.0 1.9 pad_maximum_fusion.1
  324.8 2.9 fusion.84
  327.8 3.3 copy.121
  331.6 2.2 copy.120
  333.8 1.2 collective-permute-start.4
  335.0 1.4 compare_and_fusion.7
  337.0 1.7 reduce.131
  339.3 0.7 subtract_multiply_fusion.6
  339.9 7.4 %collective-permute-done.5 = f32[9,16,48,16]{2,3,1,0:T(8,128)} collective-permute-done((f32[9,16,48,16]{2,3,1,0:T(8,128)}, f32[9,16,48,16]{2,3,1,0:T(8,128)}, u32[]{:S(2)}, u32[]{:S(2)}) %collective-permute-start.5) | collective-permute-done | bytes 442400 | tf_op jit(solution)/shard_map/ppermute | solution.py:18
  347.4 2.3 copy.123
  349.7 3.4 copy.122
  353.1 6.5 %pad_maximum_fusion = f32[9,16,48,160]{3,1,2,0:T(8,128)S(1)} fusion(f32[9,16,48,16]{3,1,2,0:T(8,128)S(1)} %copy.123, f32[9,16,16,128]{3,1,2,0:T(8,128)} %collective-permute-done.3, f32[9,16,16,128]{3,1,2,0:T(8,128)} %copy-done.1, f32[9,16,16,128]{3,1,2,0:T(8,128)} %collective-permute-done.2, f32[9,16,48,16]{3,1,2,0:T(8,128)} %copy.122), kind=kLoop, calls=%fused_computation.15 | loop fusion | flops 4423680 | bytes 8847360 | tf_op jit(solution)/shard_map/concatenate | solution.py:19
  359.7 7.4 %fusion = f32[16,9,16,160]{3,0,2,1:T(8,128)S(1)} fusion(f32[9,16,48,160]{3,1,2,0:T(8,128)S(1)} %pad_maximum_fusion, f32[48,16]{1,0:T(8,128)S(1)} %copy-done.3), kind=kOutput, calls=%fused_computation.16 | convolution fusion | flops 212340480 | bytes 5901312 | tf_op jit(solution)/shard_map/czpy,pq->czqy/dot_general | solution.py:40
  367.1 2.0 fusion.2
  369.3 1.2 stack.67
  370.5 9.0 %copy.126 = f32[6,32768]{0,1:T(8,128)} copy(f32[6,32768]{1,0:T(8,128)S(1)} %stack.67) | data formatting | bytes 1572864 | tf_op jit(solution)/shard_map/stack | solution.py:87
  379.5 16.6 %gather_fusion.11 = f32[4096,6]{1,0:T(8,128)S(1)} fusion(f32[6,32768]{0,1:T(8,128)} %copy.126, s32[4096]{0:T(1024)S(1)} %copy-done.14), kind=kCustom, calls=%fused_computation.7.clone | custom fusion | bytes 212992 | tf_op jit(solution)/shard_map/jit(_take)/gather | solution.py:59
  396.1 0.6 copy.141
  396.7 16.6 %gather_fusion.10 = f32[4096,6]{1,0:T(8,128)S(1)} fusion(f32[6,32768]{0,1:T(8,128)} %copy.126, s32[4096]{0:T(1024)S(1)} %copy-done.13), kind=kCustom, calls=%fused_computation.6.clone | custom fusion | bytes 212992 | tf_op jit(solution)/shard_map/jit(_take)/gather | solution.py:59
  413.3 0.6 copy.139
  414.0 16.8 %gather_fusion.9 = f32[4096,6]{1,0:T(8,128)S(1)} fusion(f32[6,32768]{0,1:T(8,128)} %copy.126, s32[4096]{0:T(1024)S(1)} %copy-done.12), kind=kCustom, calls=%fused_computation.5.clone | custom fusion | bytes 212992 | tf_op jit(solution)/shard_map/jit(_take)/gather | solution.py:59
  430.8 0.6 copy.137
  431.4 16.6 %gather_fusion.8 = f32[4096,6]{1,0:T(8,128)S(1)} fusion(f32[6,32768]{0,1:T(8,128)} %copy.126, s32[4096]{0:T(1024)S(1)} %copy-done.11), kind=kCustom, calls=%fused_computation.4.clone | custom fusion | bytes 212992 | tf_op jit(solution)/shard_map/jit(_take)/gather | solution.py:59
  448.0 0.6 copy.135
  448.6 16.6 %gather_fusion.7 = f32[4096,6]{1,0:T(8,128)S(1)} fusion(f32[6,32768]{0,1:T(8,128)} %copy.126, s32[4096]{0:T(1024)S(1)} %copy-done.10), kind=kCustom, calls=%fused_computation.3.clone | custom fusion | bytes 212992 | tf_op jit(solution)/shard_map/jit(_take)/gather | solution.py:59
  465.2 0.6 copy.133
  465.8 16.6 %gather_fusion.6 = f32[4096,6]{1,0:T(8,128)S(1)} fusion(f32[6,32768]{0,1:T(8,128)} %copy.126, s32[4096]{0:T(1024)S(1)} %copy-done.9), kind=kCustom, calls=%fused_computation.2.clone | custom fusion | bytes 212992 | tf_op jit(solution)/shard_map/jit(_take)/gather | solution.py:59
  483.0 16.6 %gather_fusion.5 = f32[4096,6]{1,0:T(8,128)S(1)} fusion(f32[6,32768]{0,1:T(8,128)} %copy.126, s32[4096]{0:T(1024)S(1)} %copy-done.8), kind=kCustom, calls=%fused_computation.1.clone | custom fusion | bytes 212992 | tf_op jit(solution)/shard_map/jit(_take)/gather | solution.py:59
  500.3 16.6 %gather_fusion.4 = f32[4096,6]{1,0:T(8,128)S(1)} fusion(f32[6,32768]{0,1:T(8,128)} %copy.126, s32[4096]{0:T(1024)S(1)} %copy-done.7), kind=kCustom, calls=%fused_computation.clone | custom fusion | bytes 212992 | tf_op jit(solution)/shard_map/jit(_take)/gather | solution.py:59
  518.1 0.8 reshape.701
  518.9 11.0 %all-to-all-start.2 = ((f32[64,1,384]{2,1,0:T(1,128)}), f32[64,1,384]{2,1,0:T(1,128)S(1)}, u32[]{:S(2)}, u32[]{:S(2)}) async-start(f32[64,1,384]{2,1,0:T(1,128)} %reshape.701), calls=%async_computation.2 | async-start | bytes 196608 | tf_op jit(solution)/shard_map/all_to_all | solution.py:131
  530.0 10.6 %all-to-all-done.2 = f32[64,1,384]{2,1,0:T(1,128)S(1)} async-done(((f32[64,1,384]{2,1,0:T(1,128)}), f32[64,1,384]{2,1,0:T(1,128)S(1)}, u32[]{:S(2)}, u32[]{:S(2)}) %all-to-all-start.2) | async-done | bytes 98336 | tf_op jit(solution)/shard_map/all_to_all | solution.py:131
  540.5 0.9 reduce.132
  541.6 0.7 copy.143
  542.3 2.8 gather_fusion.3
  545.3 0.8 copy.144
  (120 shorter events, 10.2 us)
Async XLA Ops:
  0.0 12.6 %copy-start = (s32[1024,1]{0,1:T(1,128)S(1)}, s32[1024,1]{0,1:T(1,128)}, u32[]{:S(2)}) copy-start(s32[1024,1]{0,1:T(1,128)} %param.9) | copy-start | bytes 12292
  1.1 28.6 %collective-permute-start = (f32[3,16,16,128]{3,1,2,0:T(8,128)S(1)}, f32[3,16,16,128]{3,1,2,0:T(8,128)S(1)}, u32[]{:S(2)}, u32[]{:S(2)}) collective-permute-start(f32[3,16,16,128]{3,1,2,0:T(8,128)S(1)} %copy.108), channel_id=1, source_target_pairs={{0,1},{1,2},{2,3},{3,0},{4,5},{5,6},{6,7},{7,4},{8,9},{9,10},{10,1... | collective-permute-start | bytes 1179656 | tf_op jit(solution)/shard_map/ppermute | solution.py:17
  3.3 26.6 %collective-permute-start.1 = (f32[3,16,16,128]{3,1,2,0:T(8,128)S(1)}, f32[3,16,16,128]{3,1,2,0:T(8,128)S(1)}, u32[]{:S(2)}, u32[]{:S(2)}) collective-permute-start(f32[3,16,16,128]{3,1,2,0:T(8,128)S(1)} %copy.108), channel_id=1, source_target_pairs={{1,0},{2,1},{3,2},{0,3},{5,4},{6,5},{7,6},{4,7},{9,8},{10,9},{11,1... | collective-permute-start | bytes 1179656 | tf_op jit(solution)/shard_map/ppermute | solution.py:18
  24.9 4.9 copy-start.4
  29.7 3.1 copy-start.2
  30.7 49.1 %copy-start.31 = (s32[1024]{0:T(1024)S(1)}, s32[1024]{0:T(1024)}, u32[]{:S(2)}) copy-start(s32[1024]{0:T(1024)} %param.11) | copy-start | bytes 12292
  30.7 49.1 %copy-start.32 = (s32[1024]{0:T(1024)S(1)}, s32[1024]{0:T(1024)}, u32[]{:S(2)}) copy-start(s32[1024]{0:T(1024)} %param.10) | copy-start | bytes 12292
  30.7 49.1 %copy-start.33 = (s32[1024]{0:T(1024)S(1)}, s32[1024]{0:T(1024)}, u32[]{:S(2)}) copy-start(s32[1024]{0:T(1024)} %param.12) | copy-start | bytes 12292
  33.3 289.7 %copy-start.1 = (f32[9,16,16,128]{3,1,2,0:T(8,128)}, f32[9,16,16,128]{3,1,2,0:T(8,128)S(1)}, u32[]{:S(2)}) copy-start(f32[9,16,16,128]{3,1,2,0:T(8,128)S(1)} %fusion.4) | copy-start | bytes 3538948
  33.3 289.7 %collective-permute-start.3 = (f32[9,16,16,128]{3,1,2,0:T(8,128)S(1)}, f32[9,16,16,128]{3,1,2,0:T(8,128)}, u32[]{:S(2)}, u32[]{:S(2)}) collective-permute-start(f32[9,16,16,128]{3,1,2,0:T(8,128)S(1)} %fusion.4), channel_id=1, source_target_pairs={{32,0},{64,32},{96,64},{128,96},{160,128},{192,160},{224,192},{0,2... | collective-permute-start | bytes 3538952 | tf_op jit(solution)/shard_map/ppermute | solution.py:18
  38.9 284.0 %collective-permute-start.2 = (f32[9,16,16,128]{3,1,2,0:T(8,128)S(1)}, f32[9,16,16,128]{3,1,2,0:T(8,128)}, u32[]{:S(2)}, u32[]{:S(2)}) collective-permute-start(f32[9,16,16,128]{3,1,2,0:T(8,128)S(1)} %fusion.4), channel_id=1, source_target_pairs={{0,32},{32,64},{64,96},{96,128},{128,160},{160,192},{192,224},{224... | collective-permute-start | bytes 3538952 | tf_op jit(solution)/shard_map/ppermute | solution.py:17
  79.8 225.2 %copy-start.28 = (s32[1024]{0:T(1024)}, s32[1024]{0:T(1024)S(1)}, u32[]{:S(2)}) copy-start(s32[1024]{0:T(1024)S(1)} %get-tuple-element.69) | copy-start | bytes 12292
  84.9 225.6 %all-to-all-start.1 = ((s32[1,64,64]{2,0,1:T(1,128)}), s32[1,64,64]{2,0,1:T(1,128)S(1)}, u32[]{:S(2)}, u32[]{:S(2)}) async-start(s32[1,64,64]{2,0,1:T(1,128)} %reshape.232), calls=%async_computation.1 | async-start | bytes 65536 | tf_op jit(solution)/shard_map/all_to_all | solution.py:114
  94.5 209.5 %copy-start.27 = (f32[3,1024]{1,0:T(4,128)S(1)}, f32[3,1024]{1,0:T(4,128)}, u32[]{:S(2)}) copy-start(f32[3,1024]{1,0:T(4,128)} %param.13) | copy-start | bytes 36868
  310.5 25.9 %all-to-all-start = ((f32[64,1,192]{2,1,0:T(1,128)}), f32[64,1,192]{2,1,0:T(1,128)}, u32[]{:S(2)}, u32[]{:S(2)}) async-start(f32[64,1,192]{2,1,0:T(1,128)} %reshape.699), calls=%async_computation | async-start | bytes 131072 | tf_op jit(solution)/shard_map/all_to_all | solution.py:121
  322.3 0.7 copy-start.6
  331.1 16.2 %collective-permute-start.5 = (f32[9,16,48,16]{2,3,1,0:T(8,128)}, f32[9,16,48,16]{2,3,1,0:T(8,128)}, u32[]{:S(2)}, u32[]{:S(2)}) collective-permute-start(f32[9,16,48,16]{2,3,1,0:T(8,128)} %copy.121), channel_id=1, source_target_pairs={{4,0},{8,4},{12,8},{16,12},{20,16},{24,20},{28,24},{0,28},{5,1},{9... | collective-permute-start | bytes 1327112 | tf_op jit(solution)/shard_map/ppermute | solution.py:18
  333.8 15.9 %collective-permute-start.4 = (f32[9,16,48,16]{2,3,1,0:T(8,128)}, f32[9,16,48,16]{2,3,1,0:T(8,128)}, u32[]{:S(2)}, u32[]{:S(2)}) collective-permute-start(f32[9,16,48,16]{2,3,1,0:T(8,128)} %copy.120), channel_id=1, source_target_pairs={{0,4},{4,8},{8,12},{12,16},{16,20},{20,24},{24,28},{28,0},{1,5},{5... | collective-permute-start | bytes 1327112 | tf_op jit(solution)/shard_map/ppermute | solution.py:17
  353.1 6.5 %copy-start.3 = (f32[48,16]{1,0:T(8,128)S(1)}, f32[48,16]{1,0:T(8,128)}, u32[]{:S(2)}) copy-start(f32[48,16]{1,0:T(8,128)} %copy-done.2) | copy-start | bytes 9220
  359.7 7.4 %copy-start.5 = (f32[20480]{0:T(1024)S(1)}, f32[20480]{0:T(1024)}, u32[]{:S(2)}) copy-start(f32[20480]{0:T(1024)} %gather_fusion.2) | copy-start | bytes 245764
  370.5 9.0 %copy-start.14 = (s32[4096]{0:T(1024)S(1)}, s32[4096]{0:T(1024)}, u32[]{:S(2)}) copy-start(s32[4096]{0:T(1024)} %get-tuple-element.103) | copy-start | bytes 49156
  379.5 17.2 %copy-start.13 = (s32[4096]{0:T(1024)S(1)}, s32[4096]{0:T(1024)}, u32[]{:S(2)}) copy-start(s32[4096]{0:T(1024)} %get-tuple-element.102) | copy-start | bytes 49156
  396.7 17.2 %copy-start.12 = (s32[4096]{0:T(1024)S(1)}, s32[4096]{0:T(1024)}, u32[]{:S(2)}) copy-start(s32[4096]{0:T(1024)} %get-tuple-element.97) | copy-start | bytes 49156
  413.9 17.4 %copy-start.11 = (s32[4096]{0:T(1024)S(1)}, s32[4096]{0:T(1024)}, u32[]{:S(2)}) copy-start(s32[4096]{0:T(1024)} %get-tuple-element.98) | copy-start | bytes 49156
  431.4 17.2 %copy-start.10 = (s32[4096]{0:T(1024)S(1)}, s32[4096]{0:T(1024)}, u32[]{:S(2)}) copy-start(s32[4096]{0:T(1024)} %get-tuple-element.99) | copy-start | bytes 49156
  448.6 17.2 %copy-start.9 = (s32[4096]{0:T(1024)S(1)}, s32[4096]{0:T(1024)}, u32[]{:S(2)}) copy-start(s32[4096]{0:T(1024)} %get-tuple-element.100) | copy-start | bytes 49156
  465.8 17.2 %copy-start.8 = (s32[4096]{0:T(1024)S(1)}, s32[4096]{0:T(1024)}, u32[]{:S(2)}) copy-start(s32[4096]{0:T(1024)} %get-tuple-element.101) | copy-start | bytes 49156
  483.0 17.3 %copy-start.7 = (s32[4096]{0:T(1024)S(1)}, s32[4096]{0:T(1024)}, u32[]{:S(2)}) copy-start(s32[4096]{0:T(1024)} %get-tuple-element.96) | copy-start | bytes 49156
  500.2 17.3 %copy-start.15 = (f32[4096]{0:T(1024)S(1)}, f32[4096]{0:T(1024)}, u32[]{:S(2)}) copy-start(f32[4096]{0:T(1024)} %get-tuple-element.80) | copy-start | bytes 49156
  500.2 17.3 %copy-start.16 = (f32[4096]{0:T(1024)S(1)}, f32[4096]{0:T(1024)}, u32[]{:S(2)}) copy-start(f32[4096]{0:T(1024)} %get-tuple-element.81) | copy-start | bytes 49156
  500.2 17.4 %copy-start.17 = (f32[4096]{0:T(1024)S(1)}, f32[4096]{0:T(1024)}, u32[]{:S(2)}) copy-start(f32[4096]{0:T(1024)} %get-tuple-element.82) | copy-start | bytes 49156
  500.2 17.4 %copy-start.18 = (f32[4096]{0:T(1024)S(1)}, f32[4096]{0:T(1024)}, u32[]{:S(2)}) copy-start(f32[4096]{0:T(1024)} %get-tuple-element.83) | copy-start | bytes 49156
  500.2 17.4 %copy-start.19 = (f32[4096]{0:T(1024)S(1)}, f32[4096]{0:T(1024)}, u32[]{:S(2)}) copy-start(f32[4096]{0:T(1024)} %get-tuple-element.84) | copy-start | bytes 49156
  500.2 17.4 %copy-start.20 = (f32[4096]{0:T(1024)S(1)}, f32[4096]{0:T(1024)}, u32[]{:S(2)}) copy-start(f32[4096]{0:T(1024)} %get-tuple-element.85) | copy-start | bytes 49156
  500.3 17.4 %copy-start.21 = (f32[4096]{0:T(1024)S(1)}, f32[4096]{0:T(1024)}, u32[]{:S(2)}) copy-start(f32[4096]{0:T(1024)} %get-tuple-element.86) | copy-start | bytes 49156
  500.3 17.4 %copy-start.22 = (f32[4096]{0:T(1024)S(1)}, f32[4096]{0:T(1024)}, u32[]{:S(2)}) copy-start(f32[4096]{0:T(1024)} %get-tuple-element.87) | copy-start | bytes 49156
  500.3 17.4 %copy-start.23 = (pred[4096]{0:T(1024)(128)(4,1)S(1)}, pred[4096]{0:T(1024)(128)(4,1)}, u32[]{:S(2)}) copy-start(pred[4096]{0:T(1024)(128)(4,1)} %get-tuple-element.92) | copy-start | bytes 12292
  500.3 17.4 %copy-start.24 = (pred[4096]{0:T(1024)(128)(4,1)S(1)}, pred[4096]{0:T(1024)(128)(4,1)}, u32[]{:S(2)}) copy-start(pred[4096]{0:T(1024)(128)(4,1)} %get-tuple-element.93) | copy-start | bytes 12292
  500.3 17.4 %copy-start.25 = (pred[4096]{0:T(1024)(128)(4,1)S(1)}, pred[4096]{0:T(1024)(128)(4,1)}, u32[]{:S(2)}) copy-start(pred[4096]{0:T(1024)(128)(4,1)} %get-tuple-element.94) | copy-start | bytes 12292
  500.3 17.4 %copy-start.26 = (pred[4096]{0:T(1024)(128)(4,1)S(1)}, pred[4096]{0:T(1024)(128)(4,1)}, u32[]{:S(2)}) copy-start(pred[4096]{0:T(1024)(128)(4,1)} %get-tuple-element.95) | copy-start | bytes 12292
  516.9 13.0 %copy-start.29 = (s32[1024]{0:T(1024)S(1)}, s32[1024]{0:T(1024)}, u32[]{:S(2)}) copy-start(s32[1024]{0:T(1024)} %copy-done.28) | copy-start | bytes 12292
  518.0 27.2 %copy-start.30 = (pred[1024]{0:T(1024)(128)(4,1)S(1)}, pred[1024]{0:T(1024)(128)(4,1)}, u32[]{:S(2)}) copy-start(pred[1024]{0:T(1024)(128)(4,1)} %get-tuple-element.68) | copy-start | bytes 3076
  518.9 21.6 %all-to-all-start.2 = ((f32[64,1,384]{2,1,0:T(1,128)}), f32[64,1,384]{2,1,0:T(1,128)S(1)}, u32[]{:S(2)}, u32[]{:S(2)}) async-start(f32[64,1,384]{2,1,0:T(1,128)} %reshape.701), calls=%async_computation.2 | async-start | bytes 196608 | tf_op jit(solution)/shard_map/all_to_all | solution.py:131
where the time goes:
time: 556 us; the launch traced here: 546 us
  local copies, waits for them, and re-layouts  409 us (74%)
  other arithmetic  63.9 us (11%)
  starting transfers between devices  42.2 us (8%)
  waiting for transfers between devices  18 us (3%)
  matrix products  12.6 us (2%)
    gather x3, local copies, waits for them, and re-layouts, band(): picked = weights[jnp.clip(offset, 0, 2 * radius)]  214 us
    gather x16, local copies, waits for them, and re-layouts, interpolate(): values = jnp.take(flat_stress, corner, axis=1)  138 us
    sub x1, other arithmetic, on_device(): sorted_rank = jnp.arange(count, dtype=jnp.int32) - starts[sorted_target]  35.9 us
  transfers between devices with their start and end apart: 9, of which 2 were waited for; matrix products, arithmetic and copies ran while one was open for 56% of the time, Pallas kernels for 0%

commit v1 on v0

--- a/solution.py
+++ b/solution.py
@@ -118,12 +118,20 @@
             concat_axis=1,
             tiled=True,
         ),
-        lax.all_to_all(
-            send_weight.reshape(3, owners, capacity),
-            ("gx", "gy"),
-            split_axis=1,
-            concat_axis=1,
-            tiled=True,
+        jnp.concatenate(
+            lax.all_to_all(
+                jnp.stack(
+                    jnp.split(
+                        send_weight.reshape(3, owners, capacity),
+                        lax.axis_size(("gx", "gy")),
+                        axis=1,
+                    )
+                ),
+                ("gx", "gy"),
+                0,
+                0,
+            ),
+            axis=1,
         ),
         size_x,
         size_y,

time: 556 us -> 642 us (1.15)
  local copies, waits for them, and re-layouts: 409 us -> 490 us
    unnamed x76 -> x213, local copies, waits for them, and re-layouts: 4.19 us -> 82.2 us
  transfers between devices with their start and end apart: 9 -> 9, of which waited for: 2 -> 2; matrix products, arithmetic and copies ran while one was open for 56% -> 62% of each run, Pallas kernels for 0% -> 0%
where the time goes in v1:
time: 642 us; the launch traced here: 631 us
  local copies, waits for them, and re-layouts  490 us (76%)
  other arithmetic  66.1 us (10%)
  starting transfers between devices  41.8 us (7%)
  waiting for transfers between devices  19.4 us (3%)
  matrix products  12.6 us (2%)
    gather x3, local copies, waits for them, and re-layouts, band(): picked = weights[jnp.clip(offset, 0, 2 * radius)]  214 us
    gather x16, local copies, waits for them, and re-layouts, interpolate(): values = jnp.take(flat_stress, corner, axis=1)  138 us
    unnamed x213, local copies, waits for them, and re-layouts  82.2 us
    sub x1, other arithmetic, on_device(): sorted_rank = jnp.arange(count, dtype=jnp.int32) - starts[sorted_target]  35.7 us
  transfers between devices with their start and end apart: 9, of which 2 were waited for; matrix products, arithmetic and copies ran while one was open for 62% of the time, Pallas kernels for 0%

profile of v1, /device:TPU:1, one launch (start us, length us, event | category | flops | bytes accessed | tf_op | source)
XLA Modules:
  0.0 631.2 jit_solution(13335636742983576505)
XLA Ops:
  0.0 1.1 copy.360
  1.1 2.2 collective-permute-start
  3.3 1.5 collective-permute-start.1
  8.9 5.1 sort.17
  14.1 4.5 gather_fusion
  18.6 4.3 compare_select_fusion.11
  23.7 35.7 %select_subtract_fusion = s32[1024]{0:T(1024)S(1)} fusion(pred[1024]{0:T(1024)(128)(4,1)S(1)} %get-tuple-element.67, pred[1024]{0:T(1024)(128)(4,1)S(1)} %get-tuple-element.66, pred[1024]{0:T(1024)(128)(4,1)S(1)} %get-tuple-element.65, pred[1024]{0:T(1024)(128)(4,1)S(1)} %get-tuple-element.64, pred[1024]{0:T(1024)(128)(4,1)S(1)} %get-tuple-element.63, ...), kind=kLoop, calls=%fused_computation.276 | loop fusion | flops 59392 | bytes 66788 | tf_op jit(solution)/shard_map/sub | solution.py:106
  59.4 4.3 scatter_custom_fusion
  64.3 4.3 scatter_custom_fusion.2
  69.3 12.8 %all-to-all-start.1 = ((s32[1,64,64]{2,0,1:T(1,128)}), s32[1,64,64]{2,0,1:T(1,128)}, u32[]{:S(2)}, u32[]{:S(2)}) async-start(s32[1,64,64]{2,0,1:T(1,128)} %reshape.235), calls=%async_computation.1 | async-start | bytes 65536 | tf_op jit(solution)/shard_map/all_to_all | solution.py:114
  82.3 4.1 scatter_custom_fusion.1
  86.4 0.8 fusion.87
  87.2 0.9 fusion.86
  89.9 0.9 copy.425
  90.8 0.8 copy.426
  91.6 0.8 copy.427
  94.1 0.8 copy.430
  95.0 0.8 copy.431
  97.5 0.8 copy.434
  100.8 0.8 copy.438
  103.3 0.8 copy.441
  104.2 0.8 copy.442
  106.7 0.8 copy.445
  107.5 0.8 copy.446
  110.0 0.8 copy.449
  110.9 0.8 copy.450
  113.4 0.8 copy.453
  163.6 4.8 gather_fusion.1
  168.7 1.1 constant_dynamic-update-slice_fusion.66
  173.1 2.9 collective-permute-start.3
  178.4 209.6 %gather_fusion.2 = f32[20480]{0:T(1024)} fusion(f32[33]{0:T(128)S(1)} %broadcast_divide_fusion, s32[20480]{0:T(1024)} %fusion.29), kind=kCustom, calls=%fused_computation.10 | custom fusion | bytes 245760 | tf_op jit(solution)/shard_map/gather | solution.py:35
  388.6 2.4 reduce.131
  391.0 1.6 reshape.702
  392.6 9.7 %all-to-all-start = ((f32[64,1,192]{2,1,0:T(1,128)}), f32[64,1,192]{2,1,0:T(1,128)}, u32[]{:S(2)}, u32[]{:S(2)}) async-start(f32[64,1,192]{2,1,0:T(1,128)} %reshape.702), calls=%async_computation | async-start | bytes 131072 | tf_op jit(solution)/shard_map/all_to_all | solution.py:122
  402.8 2.0 reduce.130
  404.9 1.4 reshape_squeeze.3
  406.3 1.4 fusion.53
  407.7 1.0 copy-done.2
  408.7 1.0 copy-done.3
  410.0 2.9 fusion.84
  412.9 3.3 copy.373
  416.8 2.2 copy.372
  418.9 1.2 collective-permute-start.4
  420.8 1.6 reduce.132
  423.7 8.8 %collective-permute-done.5 = f32[9,16,48,16]{2,3,1,0:T(8,128)} collective-permute-done((f32[9,16,48,16]{2,3,1,0:T(8,128)}, f32[9,16,48,16]{2,3,1,0:T(8,128)}, u32[]{:S(2)}, u32[]{:S(2)}) %collective-permute-start.5) | collective-permute-done | bytes 442400 | tf_op jit(solution)/shard_map/ppermute | solution.py:18
  432.5 2.3 copy.375
  434.8 3.4 copy.374
  438.3 6.5 %pad_maximum_fusion = f32[9,16,48,160]{3,1,2,0:T(8,128)S(1)} fusion(f32[9,16,48,16]{3,1,2,0:T(8,128)S(1)} %copy.375, f32[9,16,16,128]{3,1,2,0:T(8,128)} %copy-done.2, f32[9,16,16,128]{3,1,2,0:T(8,128)} %copy-done.1, f32[9,16,16,128]{3,1,2,0:T(8,128)} %copy-done.3, f32[9,16,48,16]{3,1,2,0:T(8,128)} %copy.374), kind=kLoop, calls=%fused_computation.15 | loop fusion | flops 4423680 | bytes 8847360 | tf_op jit(solution)/shard_map/concatenate | solution.py:19
  444.8 7.4 %fusion = f32[16,9,16,160]{3,0,2,1:T(8,128)S(1)} fusion(f32[9,16,48,160]{3,1,2,0:T(8,128)S(1)} %pad_maximum_fusion, f32[48,16]{1,0:T(8,128)S(1)} %copy-done.5), kind=kOutput, calls=%fused_computation.16 | convolution fusion | flops 212340480 | bytes 5901312 | tf_op jit(solution)/shard_map/czpy,pq->czqy/dot_general | solution.py:40
  452.2 2.0 fusion.2
  454.4 1.2 stack.327
  455.6 9.0 %copy.378 = f32[6,32768]{0,1:T(8,128)} copy(f32[6,32768]{1,0:T(8,128)S(1)} %stack.327) | data formatting | bytes 1572864 | tf_op jit(solution)/shard_map/stack | solution.py:87
  464.7 16.5 %gather_fusion.11 = f32[4096,6]{1,0:T(8,128)S(1)} fusion(f32[6,32768]{0,1:T(8,128)} %copy.378, s32[4096]{0:T(1024)S(1)} %copy-done.16), kind=kCustom, calls=%fused_computation.7.clone | custom fusion | bytes 212992 | tf_op jit(solution)/shard_map/jit(_take)/gather | solution.py:59
  481.8 16.6 %gather_fusion.10 = f32[4096,6]{1,0:T(8,128)S(1)} fusion(f32[6,32768]{0,1:T(8,128)} %copy.378, s32[4096]{0:T(1024)S(1)} %copy-done.15), kind=kCustom, calls=%fused_computation.6.clone | custom fusion | bytes 212992 | tf_op jit(solution)/shard_map/jit(_take)/gather | solution.py:59
  499.0 16.8 %gather_fusion.9 = f32[4096,6]{1,0:T(8,128)S(1)} fusion(f32[6,32768]{0,1:T(8,128)} %copy.378, s32[4096]{0:T(1024)S(1)} %copy-done.14), kind=kCustom, calls=%fused_computation.5.clone | custom fusion | bytes 212992 | tf_op jit(solution)/shard_map/jit(_take)/gather | solution.py:59
  516.4 16.6 %gather_fusion.8 = f32[4096,6]{1,0:T(8,128)S(1)} fusion(f32[6,32768]{0,1:T(8,128)} %copy.378, s32[4096]{0:T(1024)S(1)} %copy-done.13), kind=kCustom, calls=%fused_computation.4.clone | custom fusion | bytes 212992 | tf_op jit(solution)/shard_map/jit(_take)/gather | solution.py:59
  533.6 16.6 %gather_fusion.7 = f32[4096,6]{1,0:T(8,128)S(1)} fusion(f32[6,32768]{0,1:T(8,128)} %copy.378, s32[4096]{0:T(1024)S(1)} %copy-done.12), kind=kCustom, calls=%fused_computation.3.clone | custom fusion | bytes 212992 | tf_op jit(solution)/shard_map/jit(_take)/gather | solution.py:59
  550.8 16.6 %gather_fusion.6 = f32[4096,6]{1,0:T(8,128)S(1)} fusion(f32[6,32768]{0,1:T(8,128)} %copy.378, s32[4096]{0:T(1024)S(1)} %copy-done.11), kind=kCustom, calls=%fused_computation.2.clone | custom fusion | bytes 212992 | tf_op jit(solution)/shard_map/jit(_take)/gather | solution.py:59
  568.0 16.6 %gather_fusion.5 = f32[4096,6]{1,0:T(8,128)S(1)} fusion(f32[6,32768]{0,1:T(8,128)} %copy.378, s32[4096]{0:T(1024)S(1)} %copy-done.10), kind=kCustom, calls=%fused_computation.1.clone | custom fusion | bytes 212992 | tf_op jit(solution)/shard_map/jit(_take)/gather | solution.py:59
  585.3 16.5 %gather_fusion.4 = f32[4096,6]{1,0:T(8,128)S(1)} fusion(f32[6,32768]{0,1:T(8,128)} %copy.378, s32[4096]{0:T(1024)S(1)} %copy-done.9), kind=kCustom, calls=%fused_computation.clone | custom fusion | bytes 212992 | tf_op jit(solution)/shard_map/jit(_take)/gather | solution.py:59
  603.8 11.0 %all-to-all-start.2 = ((f32[64,1,384]{2,1,0:T(1,128)}), f32[64,1,384]{2,1,0:T(1,128)S(1)}, u32[]{:S(2)}, u32[]{:S(2)}) async-start(f32[64,1,384]{2,1,0:T(1,128)} %reshape.704), calls=%async_computation.2 | async-start | bytes 196608 | tf_op jit(solution)/shard_map/all_to_all | solution.py:139
  614.8 10.6 %all-to-all-done.2 = f32[64,1,384]{2,1,0:T(1,128)S(1)} async-done(((f32[64,1,384]{2,1,0:T(1,128)}), f32[64,1,384]{2,1,0:T(1,128)S(1)}, u32[]{:S(2)}, u32[]{:S(2)}) %all-to-all-start.2) | async-done | bytes 98336 | tf_op jit(solution)/shard_map/all_to_all | solution.py:139
  625.4 0.9 reduce.133
  627.1 2.8 gather_fusion.3
  (262 shorter events, 87.8 us)
Async XLA Ops:
  0.0 14.0 %copy-start = (s32[1024,1]{0,1:T(1,128)S(1)}, s32[1024,1]{0,1:T(1,128)}, u32[]{:S(2)}) copy-start(s32[1024,1]{0,1:T(1,128)} %param.9) | copy-start | bytes 12292
  1.1 167.5 %collective-permute-start = (f32[3,16,16,128]{3,1,2,0:T(8,128)S(1)}, f32[3,16,16,128]{3,1,2,0:T(8,128)}, u32[]{:S(2)}, u32[]{:S(2)}) collective-permute-start(f32[3,16,16,128]{3,1,2,0:T(8,128)S(1)} %copy.360), channel_id=1, source_target_pairs={{0,1},{1,2},{2,3},{3,0},{4,5},{5,6},{6,7},{7,4},{8,9},{9,10},{10,1... | collective-permute-start | bytes 1179656 | tf_op jit(solution)/shard_map/ppermute | solution.py:17
  3.3 166.5 %collective-permute-start.1 = (f32[3,16,16,128]{3,1,2,0:T(8,128)S(1)}, f32[3,16,16,128]{3,1,2,0:T(8,128)S(1)}, u32[]{:S(2)}, u32[]{:S(2)}) collective-permute-start(f32[3,16,16,128]{3,1,2,0:T(8,128)S(1)} %copy.360), channel_id=1, source_target_pairs={{1,0},{2,1},{3,2},{0,3},{5,4},{6,5},{7,6},{4,7},{9,8},{10,9},{11,1... | collective-permute-start | bytes 1179656 | tf_op jit(solution)/shard_map/ppermute | solution.py:18
  14.0 50.2 %copy-start.36 = (s32[1024]{0:T(1024)S(1)}, s32[1024]{0:T(1024)}, u32[]{:S(2)}) copy-start(s32[1024]{0:T(1024)} %param.11) | copy-start | bytes 12292
  14.0 50.2 %copy-start.37 = (s32[1024]{0:T(1024)S(1)}, s32[1024]{0:T(1024)}, u32[]{:S(2)}) copy-start(s32[1024]{0:T(1024)} %param.10) | copy-start | bytes 12292
  14.1 50.2 %copy-start.38 = (s32[1024]{0:T(1024)S(1)}, s32[1024]{0:T(1024)}, u32[]{:S(2)}) copy-start(s32[1024]{0:T(1024)} %param.12) | copy-start | bytes 12292
  14.1 68.0 %copy-start.32 = (f32[3,1024]{1,0:T(4,128)S(1)}, f32[3,1024]{1,0:T(4,128)}, u32[]{:S(2)}) copy-start(f32[3,1024]{1,0:T(4,128)} %param.13) | copy-start | bytes 36868
  64.2 23.0 %copy-start.33 = (s32[1024]{0:T(1024)}, s32[1024]{0:T(1024)S(1)}, u32[]{:S(2)}) copy-start(s32[1024]{0:T(1024)S(1)} %get-tuple-element.69) | copy-start | bytes 12292
  69.3 323.4 %all-to-all-start.1 = ((s32[1,64,64]{2,0,1:T(1,128)}), s32[1,64,64]{2,0,1:T(1,128)}, u32[]{:S(2)}, u32[]{:S(2)}) async-start(s32[1,64,64]{2,0,1:T(1,128)} %reshape.235), calls=%async_computation.1 | async-start | bytes 65536 | tf_op jit(solution)/shard_map/all_to_all | solution.py:114
  163.6 6.2 copy-start.6
  168.4 4.3 copy-start.4
  173.1 234.5 %copy-start.1 = (f32[9,16,16,128]{3,1,2,0:T(8,128)}, f32[9,16,16,128]{3,1,2,0:T(8,128)S(1)}, u32[]{:S(2)}) copy-start(f32[9,16,16,128]{3,1,2,0:T(8,128)S(1)} %fusion.4) | copy-start | bytes 3538948
  173.1 234.5 %collective-permute-start.3 = (f32[9,16,16,128]{3,1,2,0:T(8,128)S(1)}, f32[9,16,16,128]{3,1,2,0:T(8,128)S(1)}, u32[]{:S(2)}, u32[]{:S(2)}) collective-permute-start(f32[9,16,16,128]{3,1,2,0:T(8,128)S(1)} %fusion.4), channel_id=1, source_target_pairs={{32,0},{64,32},{96,64},{128,96},{160,128},{192,160},{224,192},{0,2... | collective-permute-start | bytes 3538952 | tf_op jit(solution)/shard_map/ppermute | solution.py:18
  176.0 231.6 %collective-permute-start.2 = (f32[9,16,16,128]{3,1,2,0:T(8,128)S(1)}, f32[9,16,16,128]{3,1,2,0:T(8,128)S(1)}, u32[]{:S(2)}, u32[]{:S(2)}) collective-permute-start(f32[9,16,16,128]{3,1,2,0:T(8,128)S(1)} %fusion.4), channel_id=1, source_target_pairs={{0,32},{32,64},{64,96},{96,128},{128,160},{160,192},{192,224},{224... | collective-permute-start | bytes 3538952 | tf_op jit(solution)/shard_map/ppermute | solution.py:17
  392.6 28.1 %all-to-all-start = ((f32[64,1,192]{2,1,0:T(1,128)}), f32[64,1,192]{2,1,0:T(1,128)}, u32[]{:S(2)}, u32[]{:S(2)}) async-start(f32[64,1,192]{2,1,0:T(1,128)} %reshape.702), calls=%async_computation | async-start | bytes 131072 | tf_op jit(solution)/shard_map/all_to_all | solution.py:122
  407.6 1.1 copy-start.2
  408.7 1.0 copy-start.3
  416.2 16.2 %collective-permute-start.5 = (f32[9,16,48,16]{2,3,1,0:T(8,128)}, f32[9,16,48,16]{2,3,1,0:T(8,128)}, u32[]{:S(2)}, u32[]{:S(2)}) collective-permute-start(f32[9,16,48,16]{2,3,1,0:T(8,128)} %copy.373), channel_id=1, source_target_pairs={{4,0},{8,4},{12,8},{16,12},{20,16},{24,20},{28,24},{0,28},{5,1},{9... | collective-permute-start | bytes 1327112 | tf_op jit(solution)/shard_map/ppermute | solution.py:18
  416.8 3.4 copy-start.8
  418.9 15.9 %collective-permute-start.4 = (f32[9,16,48,16]{2,3,1,0:T(8,128)}, f32[9,16,48,16]{2,3,1,0:T(8,128)}, u32[]{:S(2)}, u32[]{:S(2)}) collective-permute-start(f32[9,16,48,16]{2,3,1,0:T(8,128)} %copy.372), channel_id=1, source_target_pairs={{0,4},{4,8},{8,12},{12,16},{16,20},{20,24},{24,28},{28,0},{1,5},{5... | collective-permute-start | bytes 1327112 | tf_op jit(solution)/shard_map/ppermute | solution.py:17
  438.3 6.5 %copy-start.5 = (f32[48,16]{1,0:T(8,128)S(1)}, f32[48,16]{1,0:T(8,128)}, u32[]{:S(2)}) copy-start(f32[48,16]{1,0:T(8,128)} %copy-done.4) | copy-start | bytes 9220
  444.8 7.5 %copy-start.7 = (f32[20480]{0:T(1024)S(1)}, f32[20480]{0:T(1024)}, u32[]{:S(2)}) copy-start(f32[20480]{0:T(1024)} %gather_fusion.2) | copy-start | bytes 245764
  455.6 9.0 %copy-start.16 = (s32[4096]{0:T(1024)S(1)}, s32[4096]{0:T(1024)}, u32[]{:S(2)}) copy-start(s32[4096]{0:T(1024)} %get-tuple-element.167) | copy-start | bytes 49156
  464.7 17.2 %copy-start.15 = (s32[4096]{0:T(1024)S(1)}, s32[4096]{0:T(1024)}, u32[]{:S(2)}) copy-start(s32[4096]{0:T(1024)} %get-tuple-element.166) | copy-start | bytes 49156
  481.8 17.2 %copy-start.14 = (s32[4096]{0:T(1024)S(1)}, s32[4096]{0:T(1024)}, u32[]{:S(2)}) copy-start(s32[4096]{0:T(1024)} %get-tuple-element.161) | copy-start | bytes 49156
  499.0 17.4 %copy-start.13 = (s32[4096]{0:T(1024)S(1)}, s32[4096]{0:T(1024)}, u32[]{:S(2)}) copy-start(s32[4096]{0:T(1024)} %get-tuple-element.162) | copy-start | bytes 49156
  516.4 17.2 %copy-start.12 = (s32[4096]{0:T(1024)S(1)}, s32[4096]{0:T(1024)}, u32[]{:S(2)}) copy-start(s32[4096]{0:T(1024)} %get-tuple-element.163) | copy-start | bytes 49156
  533.6 17.2 %copy-start.11 = (s32[4096]{0:T(1024)S(1)}, s32[4096]{0:T(1024)}, u32[]{:S(2)}) copy-start(s32[4096]{0:T(1024)} %get-tuple-element.164) | copy-start | bytes 49156
  550.8 17.2 %copy-start.10 = (s32[4096]{0:T(1024)S(1)}, s32[4096]{0:T(1024)}, u32[]{:S(2)}) copy-start(s32[4096]{0:T(1024)} %get-tuple-element.165) | copy-start | bytes 49156
  568.0 17.3 %copy-start.9 = (s32[4096]{0:T(1024)S(1)}, s32[4096]{0:T(1024)}, u32[]{:S(2)}) copy-start(s32[4096]{0:T(1024)} %get-tuple-element.160) | copy-start | bytes 49156
  585.2 17.3 %copy-start.17 = (f32[4096]{0:T(1024)S(1)}, f32[4096]{0:T(1024)}, u32[]{:S(2)}) copy-start(f32[4096]{0:T(1024)} %get-tuple-element.145) | copy-start | bytes 49156
  585.2 17.3 %copy-start.18 = (f32[4096]{0:T(1024)S(1)}, f32[4096]{0:T(1024)}, u32[]{:S(2)}) copy-start(f32[4096]{0:T(1024)} %get-tuple-element.146) | copy-start | bytes 49156
  585.2 17.3 %copy-start.19 = (f32[4096]{0:T(1024)S(1)}, f32[4096]{0:T(1024)}, u32[]{:S(2)}) copy-start(f32[4096]{0:T(1024)} %get-tuple-element.147) | copy-start | bytes 49156
  585.2 17.3 %copy-start.20 = (f32[4096]{0:T(1024)S(1)}, f32[4096]{0:T(1024)}, u32[]{:S(2)}) copy-start(f32[4096]{0:T(1024)} %get-tuple-element.148) | copy-start | bytes 49156
  585.2 17.3 %copy-start.21 = (f32[4096]{0:T(1024)S(1)}, f32[4096]{0:T(1024)}, u32[]{:S(2)}) copy-start(f32[4096]{0:T(1024)} %get-tuple-element.149) | copy-start | bytes 49156
  585.2 17.3 %copy-start.22 = (f32[4096]{0:T(1024)S(1)}, f32[4096]{0:T(1024)}, u32[]{:S(2)}) copy-start(f32[4096]{0:T(1024)} %get-tuple-element.150) | copy-start | bytes 49156
  585.2 17.3 %copy-start.23 = (f32[4096]{0:T(1024)S(1)}, f32[4096]{0:T(1024)}, u32[]{:S(2)}) copy-start(f32[4096]{0:T(1024)} %get-tuple-element.151) | copy-start | bytes 49156
  585.2 17.3 %copy-start.24 = (pred[4096]{0:T(1024)(128)(4,1)S(1)}, pred[4096]{0:T(1024)(128)(4,1)}, u32[]{:S(2)}) copy-start(pred[4096]{0:T(1024)(128)(4,1)} %get-tuple-element.152) | copy-start | bytes 12292
  585.2 17.3 %copy-start.25 = (pred[4096]{0:T(1024)(128)(4,1)S(1)}, pred[4096]{0:T(1024)(128)(4,1)}, u32[]{:S(2)}) copy-start(pred[4096]{0:T(1024)(128)(4,1)} %get-tuple-element.153) | copy-start | bytes 12292
  585.2 17.3 %copy-start.26 = (pred[4096]{0:T(1024)(128)(4,1)S(1)}, pred[4096]{0:T(1024)(128)(4,1)}, u32[]{:S(2)}) copy-start(pred[4096]{0:T(1024)(128)(4,1)} %get-tuple-element.154) | copy-start | bytes 12292
  585.2 17.3 %copy-start.27 = (pred[4096]{0:T(1024)(128)(4,1)S(1)}, pred[4096]{0:T(1024)(128)(4,1)}, u32[]{:S(2)}) copy-start(pred[4096]{0:T(1024)(128)(4,1)} %get-tuple-element.155) | copy-start | bytes 12292
  585.2 17.3 %copy-start.28 = (pred[4096]{0:T(1024)(128)(4,1)S(1)}, pred[4096]{0:T(1024)(128)(4,1)}, u32[]{:S(2)}) copy-start(pred[4096]{0:T(1024)(128)(4,1)} %get-tuple-element.156) | copy-start | bytes 12292
  585.3 17.3 %copy-start.29 = (pred[4096]{0:T(1024)(128)(4,1)S(1)}, pred[4096]{0:T(1024)(128)(4,1)}, u32[]{:S(2)}) copy-start(pred[4096]{0:T(1024)(128)(4,1)} %get-tuple-element.157) | copy-start | bytes 12292
  585.3 17.3 %copy-start.30 = (pred[4096]{0:T(1024)(128)(4,1)S(1)}, pred[4096]{0:T(1024)(128)(4,1)}, u32[]{:S(2)}) copy-start(pred[4096]{0:T(1024)(128)(4,1)} %get-tuple-element.158) | copy-start | bytes 12292
  585.3 17.3 %copy-start.31 = (pred[4096]{0:T(1024)(128)(4,1)S(1)}, pred[4096]{0:T(1024)(128)(4,1)}, u32[]{:S(2)}) copy-start(pred[4096]{0:T(1024)(128)(4,1)} %get-tuple-element.159) | copy-start | bytes 12292
  601.8 13.0 %copy-start.34 = (s32[1024]{0:T(1024)S(1)}, s32[1024]{0:T(1024)}, u32[]{:S(2)}) copy-start(s32[1024]{0:T(1024)} %copy-done.33) | copy-start | bytes 12292
  602.9 27.0 %copy-start.35 = (pred[1024]{0:T(1024)(128)(4,1)S(1)}, pred[1024]{0:T(1024)(128)(4,1)}, u32[]{:S(2)}) copy-start(pred[1024]{0:T(1024)(128)(4,1)} %get-tuple-element.68) | copy-start | bytes 3076
  603.8 21.6 %all-to-all-start.2 = ((f32[64,1,384]{2,1,0:T(1,128)}), f32[64,1,384]{2,1,0:T(1,128)S(1)}, u32[]{:S(2)}, u32[]{:S(2)}) async-start(f32[64,1,384]{2,1,0:T(1,128)} %reshape.704), calls=%async_computation.2 | async-start | bytes 196608 | tf_op jit(solution)/shard_map/all_to_all | solution.py:139
